TPU v7x, 512 devices: a whole 4x8x8 slice. The times are simulated.
512 devices in a mesh: tm: 32 (over z, x), frac: 16 (over y, core).
Axes of the slice: x: 4, y: 8, z: 8, core: 2. Of those that a mesh axis runs over, the one named last changes fastest.
Arguments:
- pressure0: float32 [64, 32, 128], P('frac'), may hold values from -6 to 6
- storage: float32 [64, 32, 128], P('frac'), may hold values from 0.1 to 1
- perm_base: float32 [64, 32, 128], P('frac'), may hold values from 0.2 to 5
- leakoff: float32 [64, 32, 128], P('frac'), may hold values from 0.5 to 2
- sources: float32 [32, 64, 32, 128], P('tm', 'frac'), may hold values from -6 to 6
- export_cells: int32 [4096], P('frac'), may hold values from 0 to 16383
- inter_local: int32 [16384], P('frac'), may hold values from 0 to 16383
- trace_source: int32 [16384], P('frac'), may hold values from 0 to 4095, as said below
- inter_trans: float32 [16384], P('frac'), may hold values from 0.5 to 4
- inter_count: int32 [16], P('frac'), may hold values from 1 to 1024, 8192 in all
Outputs:
- slice_pressure: float32 [32, 64, 32, 128], P('tm', 'frac')
Inputs may be any that keep to these rules, and one draw needn't show every extreme that they name: An entry of frac index d names a slot of another frac index: trace_source // 256 differs from d. `inter_count`: the live entries of a frac index are its first ones; the largest count is 1024.
All inputs are finite; a program needn't handle non-finite values. No bound on the sum of `inter_count` on one device may be relied on, other than what follows from the above.
Results may differ from a plain program's by a relative error of at most 0.00002.
Values sent between devices are 32-bit elements; how exact they have to be, the bound alone decides.
A program may use at most 64 MiB of HBM per device.

v0:
```python
import jax
import jax.numpy as jnp
from jax import lax
from jax.sharding import PartitionSpec as P

FINE_STEPS = 4
SWEEPS = 8
COARSE_SWEEPS = 2
ITERS = 2
stress_factor = 0.15
fine_size = 0.25


def next_rows(array):
    return jnp.concatenate([array[:, 1:, :], jnp.zeros_like(array[:, :1, :])], axis=1)


def prev_rows(array):
    return jnp.concatenate([jnp.zeros_like(array[:, :1, :]), array[:, :-1, :]], axis=1)


def next_cols(array):
    return jnp.concatenate([array[:, :, 1:], jnp.zeros_like(array[:, :, :1])], axis=2)


def prev_cols(array):
    return jnp.concatenate([jnp.zeros_like(array[:, :, :1]), array[:, :, :-1]], axis=2)


def implicit(pressure, slice_source, step_size, sweeps, fields, couple):
    storage, perm_base, leakoff, tisum = fields
    permeability = perm_base * jnp.exp(stress_factor * pressure)
    row_index = lax.broadcasted_iota(jnp.int32, pressure.shape, 1)
    col_index = lax.broadcasted_iota(jnp.int32, pressure.shape, 2)
    face_rows = jnp.where(
        row_index < pressure.shape[1] - 1, 0.5 * (permeability + next_rows(permeability)), 0.0
    )
    face_cols = jnp.where(
        col_index < pressure.shape[2] - 1, 0.5 * (permeability + next_cols(permeability)), 0.0
    )
    storage_rate = storage / step_size
    diagonal_total = (
        storage_rate + leakoff + face_rows + prev_rows(face_rows) + face_cols + prev_cols(face_cols)
    )
    right_side = storage_rate * pressure + slice_source
    if couple is not None:
        diagonal_total = diagonal_total + tisum
        right_side = right_side + couple(pressure)

    def sweep(sweep_index, current):
        beside = face_rows * next_rows(current) + prev_rows(face_rows * current)
        beside = beside + face_cols * next_cols(current) + prev_cols(face_cols * current)
        return (right_side + beside) / diagonal_total

    return lax.fori_loop(0, sweeps, sweep, pressure)


def body(
    pressure0,
    storage,
    perm_base,
    leakoff,
    sources,
    export_cells,
    inter_local,
    trace_source,
    inter_trans,
    inter_count,
):
    slice_count = lax.axis_size("tm")
    slice_index = lax.axis_index("tm")
    own_source = sources[0]
    entry_index = lax.broadcasted_iota(jnp.int32, inter_local.shape, 0)
    weights = jnp.where(entry_index < inter_count[0], inter_trans, jnp.zeros_like(inter_trans))
    cell_total = pressure0.size
    tisum = (
        jnp.zeros((cell_total,), jnp.float32).at[inter_local].add(weights).reshape(pressure0.shape)
    )
    fields = (storage, perm_base, leakoff, tisum)

    def couple(current):
        flat_field = current.reshape(-1)
        exported = flat_field[export_cells]
        gathered = lax.all_gather(exported, "frac", axis=0, tiled=True)
        remote_values = gathered[trace_source]
        return (
            jnp.zeros_like(flat_field)
            .at[inter_local]
            .add(weights * remote_values)
            .reshape(current.shape)
        )

    def coarse(pressure, slice_source):
        return implicit(pressure, slice_source, fine_size * FINE_STEPS, COARSE_SWEEPS, fields, None)

    all_sources = lax.all_gather(sources, "tm", axis=0, tiled=True)

    def chain(correction, carry_zero):
        if carry_zero:
            all_corrections = jnp.zeros_like(all_sources)
        else:
            all_corrections = lax.all_gather(correction[None], "tm", axis=0, tiled=True)

        def turn(turn_index, carried):
            current, kept_state = carried
            slice_source = lax.dynamic_index_in_dim(all_sources, turn_index, 0, keepdims=False)
            added = lax.dynamic_index_in_dim(all_corrections, turn_index, 0, keepdims=False)
            current = coarse(current, slice_source) + added
            kept_state = jnp.where(slice_index == turn_index + 1, current, kept_state)
            return (current, kept_state)

        final_pair = lax.fori_loop(0, slice_count - 1, turn, (pressure0, pressure0))
        return final_pair[1]

    state = chain(jnp.zeros_like(pressure0), True)
    for iteration in range(ITERS):
        fine_pressure = state
        for step_number in range(FINE_STEPS):
            fine_pressure = implicit(fine_pressure, own_source, fine_size, SWEEPS, fields, couple)
        coarse_end = coarse(state, own_source)
        state = chain(fine_pressure - coarse_end, False)
    return state[None]


def solution(mesh):
    placed = (
        P("frac", None, None),
        P("frac", None, None),
        P("frac", None, None),
        P("frac", None, None),
        P("tm", "frac", None, None),
        P("frac"),
        P("frac"),
        P("frac"),
        P("frac"),
        P("frac"),
    )
    return jax.shard_map(
        body, mesh=mesh, in_specs=placed, out_specs=P("tm", "frac", None, None), check_vma=False
    )
```

profile of v0, /device:TPU:8, one launch (start us, length us, event | category | flops | bytes accessed | tf_op | source)
XLA Modules:
  0.0 733.0 jit_solution(9327614761849319025)
XLA Ops:
  11.1 88.0 %all-gather.22.cloned.1.call-done = f32[32,4,32,128]{3,2,1,0:T(8,128)} async-done(((f32[1,4,32,128]{3,2,1,0:T(8,128)}), f32[32,4,32,128]{3,2,1,0:T(8,128)}) %all-gather.22.cloned.1.call-update) | async-done | bytes 2097168 | tf_op jit(solution)/shard_map/all_gather | solution.py:96
  99.1 52.9 %while.235 = (s32[]{:T(128)}, f32[4,32,128]{2,1,0:T(8,128)S(1)}, f32[4,32,128]{2,1,0:T(8,128)S(1)}, f32[4,32,128]{2,1,0:T(8,128)}, f32[4,32,128]{2,1,0:T(8,128)}...) while((s32[]{:T(128)}, f32[4,32,128]{2,1,0:T(8,128)S(1)}, ...), condition=%wide.region_3.4_spmd, body=%wide.region_0.3_spmd.sunk | while | flops 392741 | bytes 2790472 | solution.py:112
  102.6 0.9 bitcast_add_fusion.20
  153.0 1.7 gather_fusion
  154.8 15.7 %all-gather.10 = f32[16,1,256]{2,1,0:T(1,128)S(1)} all-gather(f32[1,1,256]{2,1,0:T(1,128)S(1)} %bitcast.174), channel_id=2, replica_groups=mesh['tm'=32,'frac'=16] {'frac'}, dimensions={0}, use_global_device_ids=true | all-gather | bytes 17408 | tf_op jit(solution)/shard_map/all_gather | solution.py:84
  170.5 6.1 gather_fusion.1
  176.7 5.9 scatter_custom_fusion.1
  182.6 5.9 scatter_custom_fusion
  188.8 1.7 while.236
  190.5 1.7 gather_fusion.2
  192.2 16.0 %all-gather.11 = f32[16,1,256]{2,1,0:T(1,128)S(1)} all-gather(f32[1,1,256]{2,1,0:T(1,128)S(1)} %bitcast.175), channel_id=3, replica_groups=mesh['tm'=32,'frac'=16] {'frac'}, dimensions={0}, use_global_device_ids=true | all-gather | bytes 17408 | tf_op jit(solution)/shard_map/all_gather | solution.py:84
  208.2 6.1 gather_fusion.3
  214.4 5.9 scatter_custom_fusion.2
  220.6 1.7 while.237
  222.4 1.7 gather_fusion.4
  224.1 15.2 %all-gather.12 = f32[16,1,256]{2,1,0:T(1,128)S(1)} all-gather(f32[1,1,256]{2,1,0:T(1,128)S(1)} %bitcast.176), channel_id=4, replica_groups=mesh['tm'=32,'frac'=16] {'frac'}, dimensions={0}, use_global_device_ids=true | all-gather | bytes 17408 | tf_op jit(solution)/shard_map/all_gather | solution.py:84
  239.3 6.1 gather_fusion.5
  245.5 5.9 scatter_custom_fusion.3
  251.8 1.7 while.238
  253.5 1.7 gather_fusion.6
  255.2 15.1 %all-gather.13 = f32[16,1,256]{2,1,0:T(1,128)S(1)} all-gather(f32[1,1,256]{2,1,0:T(1,128)S(1)} %bitcast.177), channel_id=5, replica_groups=mesh['tm'=32,'frac'=16] {'frac'}, dimensions={0}, use_global_device_ids=true | all-gather | bytes 17408 | tf_op jit(solution)/shard_map/all_gather | solution.py:84
  270.3 6.1 gather_fusion.7
  276.5 5.9 scatter_custom_fusion.4
  283.1 1.7 while.239
  285.8 79.1 %all-gather.24.cloned.1.call-done = f32[128,32,128]{2,1,0:T(8,128)} async-done(((f32[4,32,128]{2,1,0:T(8,128)}), f32[128,32,128]{2,1,0:T(8,128)}) %all-gather.24.cloned.1.call-update) | async-done | bytes 2097168 | tf_op jit(solution)/shard_map/all_gather | solution.py:102
  364.9 77.4 %while.242 = (s32[]{:T(128)}, f32[4,32,128]{2,1,0:T(8,128)S(1)}, f32[4,32,128]{2,1,0:T(8,128)S(1)}, f32[4,32,128]{2,1,0:T(8,128)S(1)}, f32[4,32,128]{2,1,0:T(8,1...) while((s32[]{:T(128)}, f32[4,32,128]{2,1,0:T(8,128)S(1)}, ...), condition=%wide.region_22.23_spmd, body=%wide.region_19.22_spmd.sunk | while | flops 409125 | bytes 2921564 | solution.py:112
  442.4 1.7 gather_fusion.8
  444.1 15.7 %all-gather.14 = f32[16,1,256]{2,1,0:T(1,128)S(1)} all-gather(f32[1,1,256]{2,1,0:T(1,128)S(1)} %bitcast.178), channel_id=7, replica_groups=mesh['tm'=32,'frac'=16] {'frac'}, dimensions={0}, use_global_device_ids=true | all-gather | bytes 17408 | tf_op jit(solution)/shard_map/all_gather | solution.py:84
  459.8 6.1 gather_fusion.9
  466.0 5.9 scatter_custom_fusion.5
  472.3 1.7 while.243
  474.0 1.7 gather_fusion.10
  475.7 16.0 %all-gather.15 = f32[16,1,256]{2,1,0:T(1,128)S(1)} all-gather(f32[1,1,256]{2,1,0:T(1,128)S(1)} %bitcast.179), channel_id=8, replica_groups=mesh['tm'=32,'frac'=16] {'frac'}, dimensions={0}, use_global_device_ids=true | all-gather | bytes 17408 | tf_op jit(solution)/shard_map/all_gather | solution.py:84
  491.7 6.1 gather_fusion.11
  497.8 5.9 scatter_custom_fusion.6
  504.1 1.7 while.244
  505.8 1.7 gather_fusion.12
  507.6 15.2 %all-gather.16 = f32[16,1,256]{2,1,0:T(1,128)S(1)} all-gather(f32[1,1,256]{2,1,0:T(1,128)S(1)} %bitcast.180), channel_id=9, replica_groups=mesh['tm'=32,'frac'=16] {'frac'}, dimensions={0}, use_global_device_ids=true | all-gather | bytes 17408 | tf_op jit(solution)/shard_map/all_gather | solution.py:84
  522.8 6.1 gather_fusion.13
  529.0 5.9 scatter_custom_fusion.7
  535.2 1.7 while.245
  536.9 1.7 gather_fusion.14
  538.7 15.1 %all-gather.17 = f32[16,1,256]{2,1,0:T(1,128)S(1)} all-gather(f32[1,1,256]{2,1,0:T(1,128)S(1)} %bitcast.173), channel_id=10, replica_groups=mesh['tm'=32,'frac'=16] {'frac'}, dimensions={0}, use_global_device_ids=true | all-gather | bytes 17408 | tf_op jit(solution)/shard_map/all_gather | solution.py:84
  553.8 6.1 gather_fusion.15
  559.9 5.9 scatter_custom_fusion.8
  566.6 1.7 while.246
  569.0 79.4 %all-gather.26.cloned.1.call-done = f32[128,32,128]{2,1,0:T(8,128)} async-done(((f32[4,32,128]{2,1,0:T(8,128)}), f32[128,32,128]{2,1,0:T(8,128)}) %all-gather.26.cloned.1.call-update) | async-done | bytes 2097168 | tf_op jit(solution)/shard_map/all_gather | solution.py:102
  648.4 77.4 %while.249 = (s32[]{:T(128)}, f32[4,32,128]{2,1,0:T(8,128)S(1)}, f32[4,32,128]{2,1,0:T(8,128)S(1)}, f32[4,32,128]{2,1,0:T(8,128)S(1)}, f32[4,32,128]{2,1,0:T(8,1...) while((s32[]{:T(128)}, f32[4,32,128]{2,1,0:T(8,128)S(1)}, ...), condition=%wide.region_40.41_spmd, body=%wide.region_37.40_spmd.sunk | while | flops 409125 | bytes 2921564 | solution.py:112
  (1683 shorter events, 260.9 us)
Async XLA Ops:
  6.5 92.6 %all-gather.22.cloned.1.call-start = ((), (), s32[]{:S(2)}) async-start(), calls=%async_computation | async-start | bytes 2162688 | tf_op jit(solution)/shard_map/all_gather | solution.py:96
  7.4 357.5 %all-gather.24.cloned.1.call-start = ((), (), s32[]{:S(2)}) async-start(), calls=%async_computation.1 | async-start | bytes 2162688 | tf_op jit(solution)/shard_map/all_gather | solution.py:102
  170.5 6.2 copy-start.5
  170.5 18.2 %copy-start = (f32[4,32,128]{2,1,0:T(8,128)S(1)}, f32[4,32,128]{2,1,0:T(8,128)}, u32[]{:S(2)}) copy-start(f32[4,32,128]{2,1,0:T(8,128)} %get-tuple-element.2573) | copy-start | bytes 196612
  170.5 18.2 %copy-start.2 = (f32[1,4,32,128]{3,2,1,0:T(8,128)S(1)}, f32[1,4,32,128]{3,2,1,0:T(8,128)}, u32[]{:S(2)}) copy-start(f32[1,4,32,128]{3,2,1,0:T(8,128)} %param.46) | copy-start | bytes 196612
  170.5 18.2 %copy-start.4 = (f32[4,32,128]{2,1,0:T(8,128)S(1)}, f32[4,32,128]{2,1,0:T(8,128)}, u32[]{:S(2)}) copy-start(f32[4,32,128]{2,1,0:T(8,128)} %param.45) | copy-start | bytes 196612
  208.2 12.1 %copy-start.1 = (f32[4,32,128]{2,1,0:T(8,128)S(1)}, f32[4,32,128]{2,1,0:T(8,128)}, u32[]{:S(2)}) copy-start(f32[4,32,128]{2,1,0:T(8,128)} %get-tuple-element.2579) | copy-start | bytes 196612
  285.5 362.8 %all-gather.26.cloned.1.call-start = ((), (), s32[]{:S(2)}) async-start(), calls=%async_computation.2 | async-start | bytes 2162688 | tf_op jit(solution)/shard_map/all_gather | solution.py:102
  725.8 0.6 copy-start.3
Sparse Core Ops, SparseCore 0:
  10.5 88.6 all-gather.21
  285.7 79.2 all-gather.23
  569.1 79.2 all-gather.25
where the time goes:
time: 741 us; the launch traced here: 733 us
  other arithmetic  264 us (36%)
  waiting for transfers between devices  247 us (33%)
  blocking collectives  124 us (17%)
  local copies, waits for them, and re-layouts  73.4 us (10%)
  between operations  14.4 us (2%)
  loops' own time  10.6 us (1%)
    all_gather x2, waiting for transfers between devices, chain(): all_corrections = lax.all_gather(correction[None], 'tm', axis=0, tiled=True)  159 us
    all_gather x8, blocking collectives, couple(): gathered = lax.all_gather(exported, 'frac', axis=0, tiled=True)  124 us
    all_gather x1, waiting for transfers between devices, body(): all_sources = lax.all_gather(sources, 'tm', axis=0, tiled=True)  88 us
    add x94, other arithmetic, implicit(): right_side = storage_rate * pressure + slice_source  82.8 us
    select_n x93, other arithmetic, turn(): kept_state = jnp.where(slice_index == turn_index + 1, current, kept_state)  55 us
    gather x8, local copies, waits for them, and re-layouts, couple(): remote_values = gathered[trace_source]  49.2 us
    scatter-add x8, other arithmetic, couple(): return jnp.zeros_like(flat_field).at[inter_local].add(weights * remote_va...  47.6 us
    div x254, other arithmetic, sweep(): return (right_side + beside) / diagonal_total  25 us
  transfers between devices with their start and end apart: 3, of which 3 were waited for; matrix products, arithmetic and copies ran while one was open for 0% of the time, Pallas kernels for 0%

commit v1 on v0

--- a/solution.py
+++ b/solution.py
@@ -99,7 +99,10 @@
         if carry_zero:
             all_corrections = jnp.zeros_like(all_sources)
         else:
-            all_corrections = lax.all_gather(correction[None], "tm", axis=0, tiled=True)
+            all_corrections = jnp.concatenate(
+                lax.all_to_all(jnp.stack([correction[None]] * lax.axis_size("tm")), "tm", 0, 0),
+                axis=0,
+            )
 
         def turn(turn_index, carried):
             current, kept_state = carried

time: 741 us -> 640 us (0.86)
  the two profiles are of different devices: /device:TPU:8 before, /device:TPU:5 now
where the time goes in v1:
time: 640 us; the launch traced here: 635 us
  other arithmetic  210 us (33%)
  waiting for transfers between devices  182 us (28%)
  blocking collectives  128 us (20%)
  local copies, waits for them, and re-layouts  76.7 us (12%)
  between operations  14.7 us (2%)
  starting transfers between devices  12.3 us (2%)
  loops' own time  10.8 us (2%)
    all_gather x8, blocking collectives, couple(): gathered = lax.all_gather(exported, 'frac', axis=0, tiled=True)  128 us
    all_to_all x2, waiting for transfers between devices, chain(): lax.all_to_all(jnp.stack([correction[None]] * lax.axis_size('tm')), 'tm',...  99.9 us
    add x94, other arithmetic, implicit(): right_side = storage_rate * pressure + slice_source  82.8 us
    all_gather x1, waiting for transfers between devices, body(): all_sources = lax.all_gather(sources, 'tm', axis=0, tiled=True)  82.3 us
    gather x8, local copies, waits for them, and re-layouts, couple(): remote_values = gathered[trace_source]  49.2 us
    scatter-add x8, other arithmetic, couple(): return jnp.zeros_like(flat_field).at[inter_local].add(weights * remote_va...  47.6 us
    div x254, other arithmetic, sweep(): return (right_side + beside) / diagonal_total  25 us
    slice x254, other arithmetic, next_cols(): array[:, :, 1:]  20.6 us
  transfers between devices with their start and end apart: 3, of which 3 were waited for; matrix products, arithmetic and copies ran while one was open for 0% of the time, Pallas kernels for 0%

profile of v1, /device:TPU:5, one launch (start us, length us, event | category | flops | bytes accessed | tf_op | source)
XLA Modules:
  0.0 634.8 jit_solution(13973755785336166617)
XLA Ops:
  11.1 82.3 %all-gather.18.cloned.1.call-done = f32[32,4,32,128]{3,2,1,0:T(8,128)} async-done(((f32[1,4,32,128]{3,2,1,0:T(8,128)}), f32[32,4,32,128]{3,2,1,0:T(8,128)}) %all-gather.18.cloned.1.call-update) | async-done | bytes 2097168 | tf_op jit(solution)/shard_map/all_gather | solution.py:96
  93.4 52.9 %while.235 = (s32[]{:T(128)}, f32[4,32,128]{2,1,0:T(8,128)S(1)}, f32[4,32,128]{2,1,0:T(8,128)S(1)}, f32[4,32,128]{2,1,0:T(8,128)}, f32[4,32,128]{2,1,0:T(8,128)}...) while((s32[]{:T(128)}, f32[4,32,128]{2,1,0:T(8,128)S(1)}, ...), condition=%wide.region_3.4_spmd, body=%wide.region_0.3_spmd.sunk | while | flops 392741 | bytes 2790472 | solution.py:115
  147.3 1.7 gather_fusion
  149.0 21.9 %all-gather.8 = f32[16,1,256]{2,1,0:T(1,128)S(1)} all-gather(f32[1,1,256]{2,1,0:T(1,128)S(1)} %bitcast.174), channel_id=2, replica_groups=mesh['tm'=32,'frac'=16] {'frac'}, dimensions={0}, use_global_device_ids=true | all-gather | bytes 17408 | tf_op jit(solution)/shard_map/all_gather | solution.py:84
  170.9 6.2 gather_fusion.1
  177.1 5.9 scatter_custom_fusion.1
  183.1 5.9 scatter_custom_fusion
  189.2 1.7 while.236
  190.9 1.7 gather_fusion.2
  192.7 15.2 %all-gather.9 = f32[16,1,256]{2,1,0:T(1,128)S(1)} all-gather(f32[1,1,256]{2,1,0:T(1,128)S(1)} %bitcast.175), channel_id=3, replica_groups=mesh['tm'=32,'frac'=16] {'frac'}, dimensions={0}, use_global_device_ids=true | all-gather | bytes 17408 | tf_op jit(solution)/shard_map/all_gather | solution.py:84
  207.9 6.1 gather_fusion.3
  214.1 5.9 scatter_custom_fusion.2
  220.3 1.7 while.237
  222.1 1.7 gather_fusion.4
  223.8 15.1 %all-gather.10 = f32[16,1,256]{2,1,0:T(1,128)S(1)} all-gather(f32[1,1,256]{2,1,0:T(1,128)S(1)} %bitcast.176), channel_id=4, replica_groups=mesh['tm'=32,'frac'=16] {'frac'}, dimensions={0}, use_global_device_ids=true | all-gather | bytes 17408 | tf_op jit(solution)/shard_map/all_gather | solution.py:84
  238.9 6.1 gather_fusion.5
  245.0 5.9 scatter_custom_fusion.3
  251.3 1.7 while.238
  253.0 1.7 gather_fusion.6
  254.8 15.2 %all-gather.11 = f32[16,1,256]{2,1,0:T(1,128)S(1)} all-gather(f32[1,1,256]{2,1,0:T(1,128)S(1)} %bitcast.177), channel_id=5, replica_groups=mesh['tm'=32,'frac'=16] {'frac'}, dimensions={0}, use_global_device_ids=true | all-gather | bytes 17408 | tf_op jit(solution)/shard_map/all_gather | solution.py:84
  270.0 6.1 gather_fusion.7
  276.2 5.9 scatter_custom_fusion.4
  282.8 1.7 while.239
  286.2 6.6 %all-to-all-start = ((f32[32,1,4,32,128]{4,3,2,1,0:T(8,128)}), f32[32,1,4,32,128]{4,3,2,1,0:T(8,128)S(1)}, u32[]{:S(2)}, u32[]{:S(2)}) async-start(f32[32,1,4,32,128]{4,3,2,1,0:T(8,128)} %stack.6), calls=%async_computation | async-start | bytes 4194304 | tf_op jit(solution)/shard_map/all_to_all | solution.py:103
  292.8 49.9 %all-to-all-done = f32[32,1,4,32,128]{4,3,2,1,0:T(8,128)S(1)} async-done(((f32[32,1,4,32,128]{4,3,2,1,0:T(8,128)}), f32[32,1,4,32,128]{4,3,2,1,0:T(8,128)S(1)}, u32[]{:S(2)}, u32[]{:S(2)}) %all-to-all-start) | async-done | bytes 2097184 | tf_op jit(solution)/shard_map/all_to_all | solution.py:103
  342.7 51.1 %while.242 = (s32[]{:T(128)}, f32[4,32,128]{2,1,0:T(8,128)S(1)}, f32[4,32,128]{2,1,0:T(8,128)S(1)}, f32[4,32,128]{2,1,0:T(8,128)S(1)}, f32[4,32,128]{2,1,0:T(8,1...) while((s32[]{:T(128)}, f32[4,32,128]{2,1,0:T(8,128)S(1)}, ...), condition=%wide.region_22.23_spmd, body=%wide.region_19.22_spmd.sunk | while | flops 409125 | bytes 2921564 | solution.py:115
  393.9 1.7 gather_fusion.8
  395.6 15.4 %all-gather.12 = f32[16,1,256]{2,1,0:T(1,128)S(1)} all-gather(f32[1,1,256]{2,1,0:T(1,128)S(1)} %bitcast.178), channel_id=6, replica_groups=mesh['tm'=32,'frac'=16] {'frac'}, dimensions={0}, use_global_device_ids=true | all-gather | bytes 17408 | tf_op jit(solution)/shard_map/all_gather | solution.py:84
  411.1 6.1 gather_fusion.9
  417.2 5.9 scatter_custom_fusion.5
  423.5 1.7 while.243
  425.2 1.7 gather_fusion.10
  426.9 15.2 %all-gather.13 = f32[16,1,256]{2,1,0:T(1,128)S(1)} all-gather(f32[1,1,256]{2,1,0:T(1,128)S(1)} %bitcast.179), channel_id=7, replica_groups=mesh['tm'=32,'frac'=16] {'frac'}, dimensions={0}, use_global_device_ids=true | all-gather | bytes 17408 | tf_op jit(solution)/shard_map/all_gather | solution.py:84
  442.2 6.1 gather_fusion.11
  448.3 5.9 scatter_custom_fusion.6
  456.3 1.7 gather_fusion.12
  458.1 15.1 %all-gather.14 = f32[16,1,256]{2,1,0:T(1,128)S(1)} all-gather(f32[1,1,256]{2,1,0:T(1,128)S(1)} %bitcast.180), channel_id=8, replica_groups=mesh['tm'=32,'frac'=16] {'frac'}, dimensions={0}, use_global_device_ids=true | all-gather | bytes 17408 | tf_op jit(solution)/shard_map/all_gather | solution.py:84
  473.2 6.1 gather_fusion.13
  479.3 5.9 scatter_custom_fusion.7
  485.6 1.7 while.245
  487.3 1.7 gather_fusion.14
  489.0 15.2 %all-gather.15 = f32[16,1,256]{2,1,0:T(1,128)S(1)} all-gather(f32[1,1,256]{2,1,0:T(1,128)S(1)} %bitcast.173), channel_id=9, replica_groups=mesh['tm'=32,'frac'=16] {'frac'}, dimensions={0}, use_global_device_ids=true | all-gather | bytes 17408 | tf_op jit(solution)/shard_map/all_gather | solution.py:84
  504.3 6.1 gather_fusion.15
  510.4 5.9 scatter_custom_fusion.8
  517.1 1.7 while.246
  520.5 5.7 all-to-all-start.1
  526.2 49.9 %all-to-all-done.1 = f32[32,1,4,32,128]{4,3,2,1,0:T(8,128)S(1)} async-done(((f32[32,1,4,32,128]{4,3,2,1,0:T(8,128)}), f32[32,1,4,32,128]{4,3,2,1,0:T(8,128)S(1)}, u32[]{:S(2)}, u32[]{:S(2)}) %all-to-all-start.1) | async-done | bytes 2097184 | tf_op jit(solution)/shard_map/all_to_all | solution.py:103
  576.2 51.1 %while.249 = (s32[]{:T(128)}, f32[4,32,128]{2,1,0:T(8,128)S(1)}, f32[4,32,128]{2,1,0:T(8,128)S(1)}, f32[4,32,128]{2,1,0:T(8,128)S(1)}, f32[4,32,128]{2,1,0:T(8,1...) while((s32[]{:T(128)}, f32[4,32,128]{2,1,0:T(8,128)S(1)}, ...), condition=%wide.region_40.41_spmd, body=%wide.region_37.40_spmd.sunk | while | flops 409125 | bytes 2921564 | solution.py:115
  (1683 shorter events, 212.3 us)
Async XLA Ops:
  6.5 86.8 %all-gather.18.cloned.1.call-start = ((), (), s32[]{:S(2)}) async-start(), calls=%async_computation.2 | async-start | bytes 2162688 | tf_op jit(solution)/shard_map/all_gather | solution.py:96
  170.9 6.2 copy-start.5
  170.9 18.2 %copy-start = (f32[4,32,128]{2,1,0:T(8,128)S(1)}, f32[4,32,128]{2,1,0:T(8,128)}, u32[]{:S(2)}) copy-start(f32[4,32,128]{2,1,0:T(8,128)} %get-tuple-element.2571) | copy-start | bytes 196612
  170.9 18.2 %copy-start.2 = (f32[1,4,32,128]{3,2,1,0:T(8,128)S(1)}, f32[1,4,32,128]{3,2,1,0:T(8,128)}, u32[]{:S(2)}) copy-start(f32[1,4,32,128]{3,2,1,0:T(8,128)} %param.46) | copy-start | bytes 196612
  170.9 18.2 %copy-start.4 = (f32[4,32,128]{2,1,0:T(8,128)S(1)}, f32[4,32,128]{2,1,0:T(8,128)}, u32[]{:S(2)}) copy-start(f32[4,32,128]{2,1,0:T(8,128)} %param.45) | copy-start | bytes 196612
  207.9 12.1 %copy-start.1 = (f32[4,32,128]{2,1,0:T(8,128)S(1)}, f32[4,32,128]{2,1,0:T(8,128)}, u32[]{:S(2)}) copy-start(f32[4,32,128]{2,1,0:T(8,128)} %get-tuple-element.2577) | copy-start | bytes 196612
  286.2 56.5 %all-to-all-start = ((f32[32,1,4,32,128]{4,3,2,1,0:T(8,128)}), f32[32,1,4,32,128]{4,3,2,1,0:T(8,128)S(1)}, u32[]{:S(2)}, u32[]{:S(2)}) async-start(f32[32,1,4,32,128]{4,3,2,1,0:T(8,128)} %stack.6), calls=%async_computation | async-start | bytes 4194304 | tf_op jit(solution)/shard_map/all_to_all | solution.py:103
  520.5 55.7 %all-to-all-start.1 = ((f32[32,1,4,32,128]{4,3,2,1,0:T(8,128)}), f32[32,1,4,32,128]{4,3,2,1,0:T(8,128)S(1)}, u32[]{:S(2)}, u32[]{:S(2)}) async-start(f32[32,1,4,32,128]{4,3,2,1,0:T(8,128)} %stack.7), calls=%async_computation.1 | async-start | bytes 4194304 | tf_op jit(solution)/shard_map/all_to_all | solution.py:103
  627.3 0.6 copy-start.3
Sparse Core Ops, SparseCore 0:
  10.5 82.8 all-gather.17
